TPU v7x, 32 devices: a whole 2x2x4 slice. The times are simulated.
32 devices in a mesh: tok: 8 (over z, x), tp: 4 (over y, core).
Axes of the slice: x: 2, y: 2, z: 4, core: 2. Of those that a mesh axis runs over, the one named last changes fastest.
Arguments:
- tokens: bfloat16 [36928, 768], P('tok'), may hold values from -6 to 6
- slot_index: int32 [36928], P('tok'), may hold values from -1 to 18477, as said below
- segment: int32 [36928], P('tok'), may hold values from 0 to 3, as said below
- router: float32 [768], replicated, may hold values from -0.21875 to 0.21875
- first_norm: float32 [2, 768], replicated, may hold values from -0.6 to 1.3
- qkv_weight: bfloat16 [768, 3, 768], P(None, None, 'tp'), may hold values from -0.21875 to 0.21875
- qv_bias: float32 [2, 768], P(None, 'tp'), may hold values from -4 to 4
- out_weight: bfloat16 [768, 768], P('tp'), may hold values from -1.75 to 1.75
- out_bias: float32 [768], P('tp'), may hold values from -4 to 4
- second_norm: float32 [2, 768], replicated, may hold values from -0.6 to 1.3
- up_weight: bfloat16 [768, 3072], P(None, 'tp'), may hold values from -0.21875 to 0.21875
- up_bias: float32 [3072], P('tp'), may hold values from -4 to 4
- down_weight: bfloat16 [3072, 768], P('tp'), may hold values from -0.109375 to 0.109375
- down_bias: float32 [768], P('tp'), may hold values from -4 to 4
- cotangent: bfloat16 [36928, 768], P('tok'), may hold values from -6 to 6
Outputs:
- layer_out: bfloat16 [36928, 768], P('tok', 'tp')
- d_tokens: float32 [36928, 768], P('tok', 'tp')
- d_qkv_weight: float32 [768, 3, 768], P(None, None, 'tp')
- d_qv_bias: float32 [2, 768], P(None, 'tp')
- d_out_weight: float32 [768, 768], P('tp')
- d_out_bias: float32 [768], P('tp')
- d_up_weight: float32 [768, 3072], P(None, 'tp')
- d_up_bias: float32 [3072], P('tp')
- d_down_weight: float32 [3072, 768], P('tp')
- d_down_bias: float32 [768], P('tp')
- d_first_norm: float32 [2, 768], P(None, 'tp')
- d_second_norm: float32 [2, 768], P(None, 'tp')
- d_router: float32 [768], P('tp')
Inputs may be any that keep to these rules, and one draw needn't show every extreme that they name: `slot_index`: -1 where the router leaves a patch out; else a slot of the compact buffers, slot // 289 being its row buffer, owned by index slot // 2312 of tok. No slot is named twice, each buffer's named slots are its lowest ones, every index of tok holds exactly 2168 selected patches and owns 2168 named slots, and at most 271 of the selected patches of one index of tok lie in rows of one owner. `segment`: within a row buffer the segments of named slots never fall from one slot to the next.
All inputs are finite; a program needn't handle non-finite values.
Results may differ from a plain program's by a relative error of at most 0.013.
Values may be sent and summed in bfloat16 or wider, within the bound.
No kernel may reach another device: no remote copies, remote signals or barrier semaphores. Data moves between devices by JAX's collectives and lax.ppermute only.
A program may use at most 320 MiB of HBM per device.

v0:
```python
import jax
import jax.numpy as jnp
from jax import lax
from jax.sharding import PartitionSpec as P

HD = 64
ROWS_DEV = 8
SLOTS = 289


HIGHEST_PRECISION = lax.Precision.HIGHEST
EPSILON = 1e-06
MASKED_SCORE = -1000000000.0


def normalize(values, gain_row, shift_row):
    row_mean = jnp.mean(values, axis=-1, keepdims=True)
    centered = values - row_mean
    inverse = lax.rsqrt(jnp.mean(centered * centered, axis=-1, keepdims=True) + EPSILON)
    normal = centered * inverse
    return (normal * gain_row + shift_row, normal, inverse)


def norm_back(grad_in, normal, inverse, gain_row):
    scaled = grad_in * gain_row
    return inverse * (
        scaled
        - jnp.mean(scaled, axis=-1, keepdims=True)
        - normal * jnp.mean(scaled * normal, axis=-1, keepdims=True)
    )


def contract_rows(left_side, right_side):
    return lax.dot_general(
        left_side, right_side, (((0,), (0,)), ((), ())), preferred_element_type=jnp.float32
    )


def contract_cols(left_side, right_side):
    return lax.dot_general(
        left_side, right_side, (((1,), (1,)), ((), ())), preferred_element_type=jnp.float32
    )


def share_of(source, axis_dim, part_index, shares):
    piece_width = source.shape[axis_dim] // shares
    return lax.dynamic_slice_in_dim(source, part_index * piece_width, piece_width, axis_dim)


def gelu_exact(values):
    return jax.nn.gelu(values, approximate=False)


def pick_rows(source, index_rows, filler):
    return jnp.take(source, index_rows, axis=0, mode="fill", fill_value=filler)


def body(
    tokens,
    slot_index,
    segment,
    router,
    first_norm,
    qkv_weight,
    qv_bias,
    out_weight,
    out_bias,
    second_norm,
    up_weight,
    up_bias,
    down_weight,
    down_bias,
    cotangent,
):
    peer_count = lax.axis_size("tok")
    shares = lax.axis_size("tp")
    my_part = lax.axis_index("tp")
    local_count = tokens.shape[0]
    model_width = tokens.shape[1]
    share_width = model_width // shares
    inner_local = qkv_weight.shape[2]
    heads_local = inner_local // HD
    slots_owned = ROWS_DEV * SLOTS
    live_count = slots_owned - slots_owned // 16
    capacity = (live_count + peer_count - 1) // peer_count
    buffer_rows = peer_count * capacity
    score_scale = HD ** (-0.5)
    inputs = tokens.astype(jnp.float32)
    chosen = slot_index >= 0
    chosen_float = chosen.astype(jnp.float32)
    owner_index = jnp.where(chosen, slot_index // slots_owned, peer_count)
    matches = (owner_index[:, None] == jnp.arange(peer_count, dtype=jnp.int32)[None, :]).astype(
        jnp.int32
    )
    order_rank = jnp.sum(jnp.cumsum(matches, axis=0) * matches, axis=1) - 1
    placed = jnp.where(chosen, owner_index * capacity + order_rank, buffer_rows)
    local_slot = jnp.where(chosen, slot_index % slots_owned, slots_owned)
    fetch_rows = jnp.minimum(placed, buffer_rows - 1)
    source_of = (
        jnp.full((buffer_rows,), local_count, jnp.int32)
        .at[placed]
        .set(jnp.arange(local_count, dtype=jnp.int32), mode="drop")
    )
    normed, first_hat, first_inv = normalize(inputs, first_norm[0], first_norm[1])
    normed_low = normed.astype(jnp.bfloat16)
    gate_value = jax.nn.sigmoid(jnp.dot(inputs, router, precision=HIGHEST_PRECISION))
    branch_scale = chosen_float * gate_value
    send_rows = pick_rows(normed_low, source_of, 0).reshape(peer_count, capacity, model_width)
    send_slot = pick_rows(local_slot, source_of, slots_owned).reshape(peer_count, capacity)
    send_segment = pick_rows(segment, source_of, -1).reshape(peer_count, capacity)
    got_rows, got_slot, got_segment = (
        lax.all_to_all(send_rows, "tok", split_axis=0, concat_axis=0, tiled=True),
        lax.all_to_all(send_slot, "tok", split_axis=0, concat_axis=0, tiled=True),
        lax.all_to_all(send_segment, "tok", split_axis=0, concat_axis=0, tiled=True),
    )
    feature_rows = got_rows.reshape(buffer_rows, model_width)
    slot_rows = got_slot.reshape(buffer_rows)
    segment_rows = got_segment.reshape(buffer_rows)
    slot_source = (
        jnp.full((slots_owned,), buffer_rows, jnp.int32)
        .at[slot_rows]
        .set(jnp.arange(buffer_rows, dtype=jnp.int32), mode="drop")
    )
    flat_weight = qkv_weight.reshape(model_width, 3 * inner_local)
    projected = jnp.dot(feature_rows, flat_weight, preferred_element_type=jnp.float32).reshape(
        buffer_rows, 3, inner_local
    )
    bias_rows = jnp.stack([qv_bias[0], jnp.zeros_like(qv_bias[0]), qv_bias[1]])
    projected_low = (
        (projected + bias_rows[None]).astype(jnp.bfloat16).reshape(buffer_rows, 3 * inner_local)
    )
    slot_qkv = pick_rows(projected_low, slot_source, 0).reshape(slots_owned, 3, inner_local)
    slot_segment = pick_rows(segment_rows, slot_source, -1).reshape(ROWS_DEV, SLOTS)
    allowed = (slot_segment[:, :, None] == slot_segment[:, None, :]) & (
        slot_segment[:, None, :] >= 0
    )
    grouped = slot_qkv.reshape(ROWS_DEV, SLOTS, 3, heads_local, HD)
    query_low = grouped[:, :, 0]
    key_low = grouped[:, :, 1]
    value_low = grouped[:, :, 2]

    def masked_scores():
        raw_scores = (
            jnp.einsum("rqhe,rkhe->rhqk", query_low, key_low, preferred_element_type=jnp.float32)
            * score_scale
        )
        return jnp.where(allowed[:, None], raw_scores, MASKED_SCORE)

    scores = masked_scores()
    top_score = jnp.max(scores, axis=-1, keepdims=True)
    log_total = top_score + jnp.log(jnp.sum(jnp.exp(scores - top_score), axis=-1, keepdims=True))
    attention_weights = jnp.exp(scores - log_total)
    attended = jnp.einsum(
        "rhqk,rkhe->rqhe",
        attention_weights.astype(jnp.bfloat16),
        value_low,
        preferred_element_type=jnp.float32,
    )
    heads_low = attended.reshape(slots_owned, inner_local).astype(jnp.bfloat16)
    heads_rows = pick_rows(heads_low, slot_rows, 0)
    bias_full = lax.dynamic_update_slice(
        jnp.zeros((model_width,), jnp.float32), out_bias, (my_part * share_width,)
    )
    out_part = (
        jnp.dot(heads_rows, out_weight, preferred_element_type=jnp.float32) + bias_full[None, :]
    )
    returned_sum = lax.psum(out_part, "tp")
    returned_low = returned_sum.astype(jnp.bfloat16).reshape(peer_count, capacity, model_width)
    came_back = lax.all_to_all(
        returned_low, "tok", split_axis=0, concat_axis=0, tiled=True
    ).reshape(buffer_rows, model_width)
    branch = jnp.take(came_back, fetch_rows, axis=0).astype(jnp.float32)
    residual = inputs + branch_scale[:, None] * branch
    second_in, second_hat, second_inv = normalize(residual, second_norm[0], second_norm[1])
    second_low = second_in.astype(jnp.bfloat16)
    pre_hidden = jnp.dot(second_low, up_weight, preferred_element_type=jnp.float32) + up_bias
    hidden_low = gelu_exact(pre_hidden).astype(jnp.bfloat16)
    mixer_part = jnp.dot(hidden_low, down_weight, preferred_element_type=jnp.float32)
    mixer_share = lax.psum_scatter(
        mixer_part.astype(jnp.bfloat16), "tp", scatter_dimension=1, tiled=True
    ).astype(jnp.float32)
    layer_out = (mixer_share + share_of(residual, 1, my_part, shares) + down_bias).astype(
        jnp.bfloat16
    )
    cot_float = cotangent.astype(jnp.float32)
    d_down_weight = contract_rows(hidden_low, cotangent)
    d_down_bias = jnp.sum(share_of(cot_float, 1, my_part, shares), axis=0)
    d_hidden = contract_cols(cotangent, down_weight)
    gelu_pull = jax.vjp(gelu_exact, pre_hidden)[1]
    d_pre = gelu_pull(d_hidden)[0].astype(jnp.bfloat16)
    d_up_weight = contract_rows(second_low, d_pre)
    d_up_bias = jnp.sum(d_pre.astype(jnp.float32), axis=0)
    norm_part = contract_cols(d_pre, up_weight)
    norm_share = lax.psum_scatter(norm_part, "tp", scatter_dimension=1, tiled=True)
    d_second = lax.all_gather(norm_share, "tp", axis=1, tiled=True)
    d_residual = cot_float + norm_back(d_second, second_hat, second_inv, second_norm[0])
    second_share = share_of(second_hat, 1, my_part, shares)
    d_second_norm = jnp.stack(
        [jnp.sum(norm_share * second_share, axis=0), jnp.sum(norm_share, axis=0)]
    )
    d_branch = (d_residual * branch_scale[:, None]).astype(jnp.bfloat16)
    d_gate = jnp.sum(d_residual * branch, axis=1)
    d_logit = d_gate * gate_value * (1.0 - gate_value) * chosen_float
    d_router = jnp.dot(d_logit, share_of(inputs, 1, my_part, shares), precision=HIGHEST_PRECISION)
    d_out_bias = jnp.sum(share_of(d_branch, 1, my_part, shares).astype(jnp.float32), axis=0)
    send_grad = pick_rows(d_branch, source_of, 0).reshape(peer_count, capacity, model_width)
    grad_rows = lax.all_to_all(send_grad, "tok", split_axis=0, concat_axis=0, tiled=True).reshape(
        buffer_rows, model_width
    )
    d_out_weight = contract_rows(heads_rows, grad_rows)
    d_heads = contract_cols(grad_rows, out_weight).astype(jnp.bfloat16)
    slot_dheads = pick_rows(d_heads, slot_source, 0).reshape(ROWS_DEV, SLOTS, heads_local, HD)
    again_scores = masked_scores()
    again_weights = jnp.exp(again_scores - log_total)
    weights_low = again_weights.astype(jnp.bfloat16)
    d_weights = jnp.einsum(
        "rqhe,rkhe->rhqk", slot_dheads, value_low, preferred_element_type=jnp.float32
    )
    d_value = jnp.einsum(
        "rhqk,rqhe->rkhe", weights_low, slot_dheads, preferred_element_type=jnp.float32
    )
    d_scores = (
        again_weights * (d_weights - jnp.sum(again_weights * d_weights, axis=-1, keepdims=True))
    ).astype(jnp.bfloat16)
    d_query = (
        jnp.einsum("rhqk,rkhe->rqhe", d_scores, key_low, preferred_element_type=jnp.float32)
        * score_scale
    )
    d_key = (
        jnp.einsum("rhqk,rqhe->rkhe", d_scores, query_low, preferred_element_type=jnp.float32)
        * score_scale
    )
    d_slots = (
        jnp.stack([d_query, d_key, d_value], axis=2)
        .astype(jnp.bfloat16)
        .reshape(slots_owned, 3, inner_local)
    )
    d_rows = pick_rows(d_slots, slot_rows, 0)
    d_flat = d_rows.reshape(buffer_rows, 3 * inner_local)
    d_qkv_weight = contract_rows(feature_rows, d_flat).reshape(model_width, 3, inner_local)
    d_qv_bias = jnp.stack(
        [
            jnp.sum(d_rows[:, 0].astype(jnp.float32), axis=0),
            jnp.sum(d_rows[:, 2].astype(jnp.float32), axis=0),
        ]
    )
    feature_part = contract_cols(d_flat, flat_weight)
    feature_sum = lax.psum(feature_part, "tp")
    feature_low = feature_sum.astype(jnp.bfloat16).reshape(peer_count, capacity, model_width)
    feature_back = lax.all_to_all(
        feature_low, "tok", split_axis=0, concat_axis=0, tiled=True
    ).reshape(buffer_rows, model_width)
    d_normed = (
        jnp.take(feature_back, fetch_rows, axis=0).astype(jnp.float32) * chosen_float[:, None]
    )
    d_inputs = (
        d_residual
        + norm_back(d_normed, first_hat, first_inv, first_norm[0])
        + d_logit[:, None] * router[None, :]
    )
    normed_share = share_of(d_normed, 1, my_part, shares)
    d_first_norm = jnp.stack(
        [
            jnp.sum(normed_share * share_of(first_hat, 1, my_part, shares), axis=0),
            jnp.sum(normed_share, axis=0),
        ]
    )
    totals = lax.psum(
        (
            d_qkv_weight,
            d_qv_bias,
            d_out_weight,
            d_out_bias,
            d_up_weight,
            d_up_bias,
            d_down_weight,
            d_down_bias,
            d_first_norm,
            d_second_norm,
            d_router,
        ),
        "tok",
    )
    return (
        layer_out,
        share_of(d_inputs, 1, my_part, shares),
        totals[0],
        totals[1],
        totals[2],
        totals[3],
        totals[4],
        totals[5],
        totals[6],
        totals[7],
        totals[8],
        totals[9],
        totals[10],
    )


def solution(mesh):
    return jax.shard_map(
        body,
        mesh=mesh,
        in_specs=(
            P("tok", None),
            P("tok"),
            P("tok"),
            P(),
            P(),
            P(None, None, "tp"),
            P(None, "tp"),
            P("tp", None),
            P("tp"),
            P(),
            P(None, "tp"),
            P("tp"),
            P("tp", None),
            P("tp"),
            P("tok", None),
        ),
        out_specs=(
            P("tok", "tp"),
            P("tok", "tp"),
            P(None, None, "tp"),
            P(None, "tp"),
            P("tp", None),
            P("tp"),
            P(None, "tp"),
            P("tp"),
            P("tp", None),
            P("tp"),
            P(None, "tp"),
            P(None, "tp"),
            P("tp"),
        ),
        check_vma=False,
    )
```

profile of v0, /device:TPU:0, one launch (start us, length us, event | category | flops | bytes accessed | tf_op | source)
XLA Modules:
  0.0 1572.0 jit_solution(8899263688292350029)
XLA Ops:
  13.3 22.9 %scatter_custom_fusion = s32[2168]{0:T(1024)S(1)} fusion(s32[4616]{0:T(1024)S(1)} %get-tuple-element.63, s32[4616]{0:T(1024)S(1)} %iota.11, s32[]{:T(128)} %constant.99.clone.1), kind=kCustom, calls=%fused_computation.160 | custom fusion | bytes 8676 | tf_op jit(solution)/shard_map/scatter | solution.py:102
  103.9 13.3 gather_fusion.7
  117.2 16.8 %all-to-all-start.2 = ((s32[8,1,271]{2,1,0:T(1,128)}), s32[8,1,271]{2,1,0:T(1,128)S(1)}, u32[]{:S(2)}, u32[]{:S(2)}) async-start(s32[8,1,271]{2,1,0:T(1,128)} %select_n.168), calls=%async_computation.2 | async-start | bytes 24576 | tf_op jit(solution)/shard_map/all_to_all | solution.py:114
  160.5 12.7 gather_fusion.3
  174.4 47.9 %all-to-all-done.1 = bf16[8,271,768]{2,1,0:T(8,128)(2,1)} async-done(((bf16[8,271,768]{2,1,0:T(8,128)(2,1)}), bf16[8,271,768]{2,1,0:T(8,128)(2,1)}, u32[]{:S(2)}, u32[]{:S(2)}) %all-to-all-start.1) | async-done | bytes 3330080 | tf_op jit(solution)/shard_map/all_to_all | solution.py:112
  248.3 13.5 reshape.455
  305.0 117.6 %all-reduce.8 = bf16[2168,768]{1,0:T(8,128)(2,1)} all-reduce(f32[2168,768]{1,0:T(8,128)} %convolution_add_fusion), channel_id=1, replica_groups=mesh['tok'=8,'tp'=4] {'tp'}, use_global_device_ids=true, to_apply=%region_9.11 | all-reduce | flops 1665024 | bytes 9990144 | tf_op jit(solution)/shard_map/psum | solution.py:167
  441.8 66.1 %all-to-all-done.3 = bf16[8,271,768]{2,1,0:T(8,128)(2,1)} async-done(((bf16[8,271,768]{2,1,0:T(8,128)(2,1)}), bf16[8,271,768]{2,1,0:T(8,128)(2,1)}, u32[]{:S(2)}, u32[]{:S(2)}) %all-to-all-start.3) | async-done | bytes 3330080 | tf_op jit(solution)/shard_map/all_to_all | solution.py:169
  512.4 20.7 %gather_fusion.8 = bf16[4616,768]{1,0:T(8,128)(2,1)} fusion(bf16[2168,768]{1,0:T(8,128)(2,1)} %reshape.320, s32[5120]{0:T(1024)S(1)} %pad_clamp_fusion), kind=kCustom, calls=%fused_computation.1.clone | custom fusion | bytes 14198816 | tf_op jit(solution)/shard_map/jit(_take)/gather | solution.py:172
  543.1 13.1 fusion.48
  581.0 40.5 %convert_reduce_fusion.1 = (f32[768]{0:T(1024)}, bf16[4616,768]{1,0:T(8,128)(2,1)}, f32[4616,768]{1,0:T(8,128)}) fusion(f32[4616,768]{1,0:T(8,128)S(1)} %fusion.50, f32[768]{0:T(1024)S(1)} %copy-done.58, bf16[4616,768]{1,0:T(8,128)(2,1)S(1)} %bitcast.94, bf16[768,768]{1,0:T(8,128)(2,1)S(1)} %copy-done), kind=kOutput, calls=%fused_computation.32 | convolution fusion | flops 5711135744 | bytes 43726848 | tf_op jit(solution)/shard_map/dot_general | solution.py:40
  633.3 111.4 %reduce-scatter.5.cloned.1.call-done = f32[4616,192]{0,1:T(8,128)} async-done(((f32[4616,768]{0,1:T(8,128)}), f32[4616,192]{0,1:T(8,128)}) %reduce-scatter.5.cloned.1.call-update) | async-done | bytes 3545104 | tf_op jit(solution)/shard_map/reduce_scatter | solution.py:194
  755.0 84.5 %all-gather.2.cloned.1.call-done = f32[4616,768]{0,1:T(8,128)} async-done(((f32[4616,192]{0,1:T(8,128)}), f32[4616,768]{0,1:T(8,128)}) %all-gather.2.cloned.1.call-update) | async-done | bytes 14180368 | tf_op jit(solution)/shard_map/all_gather | solution.py:195
  839.5 12.2 multiply_reduce_fusion.3
  855.2 14.0 multiply_convert_fusion
  879.6 13.3 gather_fusion.9
  939.8 42.4 %all-to-all-done.4 = bf16[8,271,768]{2,1,0:T(8,128)(2,1)} async-done(((bf16[8,271,768]{2,1,0:T(8,128)(2,1)}), bf16[8,271,768]{2,1,0:T(8,128)(2,1)}, u32[]{:S(2)}, u32[]{:S(2)}) %all-to-all-start.4) | async-done | bytes 3330080 | tf_op jit(solution)/shard_map/all_to_all | solution.py:207
  1094.3 13.1 gather_fusion.6
  1125.4 118.2 %all-reduce.9 = bf16[2168,768]{1,0:T(8,128)(2,1)} all-reduce(f32[2168,768]{1,0:T(8,128)} %convolution_bitcast_fusion), channel_id=1, replica_groups=mesh['tok'=8,'tp'=4] {'tp'}, use_global_device_ids=true, to_apply=%region_17.20 | all-reduce | flops 1665024 | bytes 9990144 | tf_op jit(solution)/shard_map/psum | solution.py:248
  1307.1 64.3 %all-to-all-done.5 = bf16[8,271,768]{2,1,0:T(8,128)(2,1)} async-done(((bf16[8,271,768]{2,1,0:T(8,128)(2,1)}), bf16[8,271,768]{2,1,0:T(8,128)(2,1)}, u32[]{:S(2)}, u32[]{:S(2)}) %all-to-all-start.5) | async-done | bytes 3330080 | tf_op jit(solution)/shard_map/all_to_all | solution.py:250
  1376.1 20.9 %gather_fusion.10 = bf16[4616,768]{1,0:T(8,128)(2,1)} fusion(bf16[2168,768]{1,0:T(8,128)(2,1)} %reshape.324, s32[5120]{0:T(1024)S(1)} %copy-done.42), kind=kCustom, calls=%fused_computation.3.clone | custom fusion | bytes 14198816 | tf_op jit(solution)/shard_map/jit(_take)/gather | solution.py:254
  1407.2 27.1 %fusion.45 = (f32[4616]{0:T(1024)S(1)}, f32[4616]{0:T(1024)S(1)}, f32[4616]{0:T(1024)S(1)}, f32[4616,768]{0,1:T(8,128)}, f32[4616,768]{0,1:T(8,128)}, /*index=5*/f32[4616,768]{0,1:T(8,128)}) fusion(f32[768]{0:T(1024)S(1)} %copy-done.54, f32[4616]{0:T(1024)S(1)} %copy-done.44, bf16[4616,768]{0,1:T(8,128)(2,1)} %copy.95, pred[4616]{0:T(1024)(128)(4,1)S(1)} %copy-done.52, ...), kind=kLoop, calls=%fused_computation.173 | loop fusion | flops 49617384 | bytes 78110408 | tf_op jit(solution)/shard_map/reduce_sum | solution.py:28
  1446.9 45.7 %all-reduce.1 = (f32[2,192]{1,0:T(2,128)}, f32[192]{0:T(256)}, f32[768]{0:T(1024)}, f32[192]{0:T(256)}, f32[2,192]{1,0:T(2,128)}, /*index=5*/f32[2,192]{1,0:T(2,128)}, f32[192]{0:T(256)}) all-reduce(f32[2,192]{1,0:T(2,128)S(1)} %pad_maximum_fusion.2, f32[192]{0:T(256)S(1)} %convert_reduce_fusion.2, ...), channel_id=1, replica_groups=mesh['tok'=8,'tp'=4] {'tok'}, use_global_device_ids=true, to_apply=%region_24.27 | all-reduce | flops 2496 | bytes 19968 | tf_op jit(solution)/shard_map/psum | solution.py:268
  1492.6 63.2 %all-reduce.7.cloned.1.call-done = (f32[768,3,192]{0,2,1:T(8,128)}, f32[192,768]{1,0:T(8,128)}, f32[768,768]{1,0:T(8,128)}, f32[768,768]{1,0:T(8,128)}) async-done(((f32[768,3,192]{0,2,1:T(8,128)}, f32[192,768]{1,0:T(8,128)}, f32[768,768]{1,0:T(8,128)}, f32[768,768]{1,0:T(8,128)}), (f32[768,3,192]{0,2,1:T(8,128)}, f32[192,768]{1,0:T(8,128)}, f32[768,768]{1,0:T(8,128)}, ...) | async-done | bytes 7077904 | tf_op jit(solution)/shard_map/psum | solution.py:268
  (306 shorter events, 541.5 us)
Async XLA Ops:
  7.2 573.7 %copy-start = (bf16[768,768]{1,0:T(8,128)(2,1)S(1)}, bf16[768,768]{1,0:T(8,128)(2,1)}, u32[]{:S(2)}) copy-start(bf16[768,768]{1,0:T(8,128)(2,1)} %param.31) | copy-start | bytes 3538948
  8.6 432.5 %copy-start.39 = (pred[4616]{0:T(1024)(128)(4,1)}, pred[4616]{0:T(1024)(128)(4,1)S(1)}, u32[]{:S(2)}) copy-start(pred[4616]{0:T(1024)(128)(4,1)S(1)} %get-tuple-element.47) | copy-start | bytes 13852
  36.3 67.6 %copy-start.28 = (s32[3072]{0:T(1024)}, s32[3072]{0:T(1024)S(1)}, u32[]{:S(2)}) copy-start(s32[3072]{0:T(1024)S(1)} %pad_clamp_fusion.3) | copy-start | bytes 36868
  59.8 74.2 %copy-start.49 = (pred[2168]{0:T(1024)(128)(4,1)}, pred[2168]{0:T(1024)(128)(4,1)S(1)}, u32[]{:S(2)}) copy-start(pred[2168]{0:T(1024)(128)(4,1)S(1)} %get-tuple-element.57) | copy-start | bytes 6508
  60.5 56.7 %all-to-all-start = ((s32[8,1,271]{2,1,0:T(1,128)}), s32[8,1,271]{2,1,0:T(1,128)S(1)}, u32[]{:S(2)}, u32[]{:S(2)}) async-start(s32[8,1,271]{2,1,0:T(1,128)} %select_n.162), calls=%async_computation | async-start | bytes 24576 | tf_op jit(solution)/shard_map/all_to_all | solution.py:113
  117.2 25.2 %all-to-all-start.2 = ((s32[8,1,271]{2,1,0:T(1,128)}), s32[8,1,271]{2,1,0:T(1,128)S(1)}, u32[]{:S(2)}, u32[]{:S(2)}) async-start(s32[8,1,271]{2,1,0:T(1,128)} %select_n.168), calls=%async_computation.2 | async-start | bytes 24576 | tf_op jit(solution)/shard_map/all_to_all | solution.py:114
  142.4 79.9 %all-to-all-start.1 = ((bf16[8,271,768]{2,1,0:T(8,128)(2,1)}), bf16[8,271,768]{2,1,0:T(8,128)(2,1)}, u32[]{:S(2)}, u32[]{:S(2)}) async-start(bf16[8,271,768]{2,1,0:T(8,128)(2,1)} %reshape.314), calls=%async_computation.1 | async-start | bytes 6684672 | tf_op jit(solution)/shard_map/all_to_all | solution.py:112
  160.5 111.4 %copy-start.47 = (pred[8,289]{1,0:T(8,128)(4,1)}, pred[8,289]{1,0:T(8,128)(4,1)S(1)}, u32[]{:S(2)}) copy-start(pred[8,289]{1,0:T(8,128)(4,1)S(1)} %broadcast_in_dim.156) | copy-start | bytes 6940
  160.5 76.7 %copy-start.31 = (s32[3072]{0:T(1024)}, s32[3072]{0:T(1024)S(1)}, u32[]{:S(2)}) copy-start(s32[3072]{0:T(1024)S(1)} %pad_clamp_fusion.2) | copy-start | bytes 36868
  173.3 119.5 %copy-start.43 = (s32[3072]{0:T(1024)}, s32[3072]{0:T(1024)S(1)}, u32[]{:S(2)}) copy-start(s32[3072]{0:T(1024)S(1)} %pad_clamp_fusion.1) | copy-start | bytes 36868
  173.4 126.6 %copy-start.45 = (pred[2168]{0:T(1024)(128)(4,1)}, pred[2168]{0:T(1024)(128)(4,1)S(1)}, u32[]{:S(2)}) copy-start(pred[2168]{0:T(1024)(128)(4,1)S(1)} %compare_and_fusion.3) | copy-start | bytes 6508
  174.4 105.3 %copy-start.9 = (pred[8,289,289]{1,2,0:T(8,128)(4,1)}, pred[8,289,289]{1,2,0:T(8,128)(4,1)S(1)}, u32[]{:S(2)}) copy-start(pred[8,289,289]{1,2,0:T(8,128)(4,1)S(1)} %compare_and_fusion) | copy-start | bytes 2004508
  299.9 122.7 %copy-start.15 = (bf16[2168,192]{1,0:T(8,128)(2,1)}, bf16[2168,192]{1,0:T(8,128)(2,1)S(1)}, u32[]{:S(2)}) copy-start(bf16[2168,192]{1,0:T(8,128)(2,1)S(1)} %gather_fusion.4) | copy-start | bytes 2497540
  427.3 80.5 %all-to-all-start.3 = ((bf16[8,271,768]{2,1,0:T(8,128)(2,1)}), bf16[8,271,768]{2,1,0:T(8,128)(2,1)}, u32[]{:S(2)}, u32[]{:S(2)}) async-start(bf16[8,271,768]{2,1,0:T(8,128)(2,1)} %reshape.319), calls=%async_computation.3 | async-start | bytes 6684672 | tf_op jit(solution)/shard_map/all_to_all | solution.py:169
  432.3 312.3 %reduce-scatter.5.cloned.1.call-start = ((), (), s32[]{:S(2)}) async-start(), calls=%async_computation.9 | async-start | bytes 18186240 | tf_op jit(solution)/shard_map/reduce_scatter | solution.py:194
  432.4 110.7 %copy-start.51 = (pred[4616]{0:T(1024)(128)(4,1)}, pred[4616]{0:T(1024)(128)(4,1)S(1)}, u32[]{:S(2)}) copy-start(pred[4616]{0:T(1024)(128)(4,1)S(1)} %get-tuple-element.52) | copy-start | bytes 13852
  432.5 80.0 %copy-start.41 = (s32[5120]{0:T(1024)}, s32[5120]{0:T(1024)S(1)}, u32[]{:S(2)}) copy-start(s32[5120]{0:T(1024)S(1)} %pad_clamp_fusion) | copy-start | bytes 61444
  441.7 101.3 %copy-start.35 = (f32[4616]{0:T(1024)}, f32[4616]{0:T(1024)S(1)}, u32[]{:S(2)}) copy-start(f32[4616]{0:T(1024)S(1)} %broadcast_select_fusion.9) | copy-start | bytes 55396
  633.2 206.3 %all-gather.2.cloned.1.call-start = ((), (), s32[]{:S(2)}) async-start(), calls=%async_computation.10 | async-start | bytes 18186240 | tf_op jit(solution)/shard_map/all_gather | solution.py:195
  901.3 81.0 %all-to-all-start.4 = ((bf16[8,271,768]{2,1,0:T(8,128)(2,1)}), bf16[8,271,768]{2,1,0:T(8,128)(2,1)}, u32[]{:S(2)}, u32[]{:S(2)}) async-start(bf16[8,271,768]{2,1,0:T(8,128)(2,1)} %reshape.321), calls=%async_computation.6 | async-start | bytes 6684672 | tf_op jit(solution)/shard_map/all_to_all | solution.py:207
  906.8 386.2 %reduce-scatter.3.cloned.1.call-start = ((), (), s32[]{:S(2)}) async-start(), calls=%async_computation.8 | async-start | bytes 9093120 | tf_op jit(solution)/shard_map/reduce_scatter | solution.py:179
  1248.2 123.2 %all-to-all-start.5 = ((bf16[8,271,768]{2,1,0:T(8,128)(2,1)}), bf16[8,271,768]{2,1,0:T(8,128)(2,1)}, u32[]{:S(2)}, u32[]{:S(2)}) async-start(bf16[8,271,768]{2,1,0:T(8,128)(2,1)} %reshape.323), calls=%async_computation.7 | async-start | bytes 6684672 | tf_op jit(solution)/shard_map/all_to_all | solution.py:250
  1252.7 303.1 %all-reduce.7.cloned.1.call-start = ((), (), s32[]{:S(2)}) async-start(), calls=%async_computation.11 | async-start | bytes 14155776 | tf_op jit(solution)/shard_map/psum | solution.py:268
  1300.2 75.9 %copy-start.42 = (s32[5120]{0:T(1024)S(1)}, s32[5120]{0:T(1024)}, u32[]{:S(2)}) copy-start(s32[5120]{0:T(1024)} %copy-done.41) | copy-start | bytes 61444
  (60 other events, 879.4 us)
Sparse Core Ops, SparseCore 0:
  633.3 111.2 reduce-scatter.4
  746.2 93.2 all-gather.1
  928.6 65.3 reduce-scatter.2
  1280.4 275.3 all-reduce.6
where the time goes:
time: 1570 us
  waiting for transfers between devices  480 us (31%)
  local copies, waits for them, and re-layouts  390 us (25%)
  blocking collectives  281 us (18%)
  other arithmetic  197 us (13%)
  matrix products  164 us (10%)
  starting transfers between devices  45.6 us (3%)
    gather x15, local copies, waits for them, and re-layouts, pick_rows(): return jnp.take(source, index_rows, axis=0, mode='fill', fill_value=filler)  137 us
    psum x1, blocking collectives, body(): feature_sum = lax.psum(feature_part, 'tp')  118 us
    psum x1, blocking collectives, body(): returned_sum = lax.psum(out_part, 'tp')  118 us
    reduce_scatter x1, waiting for transfers between devices, body(): lax.psum_scatter(norm_part, 'tp', scatter_dimension=1, tiled=True)  111 us
    all_gather x1, waiting for transfers between devices, body(): d_second = lax.all_gather(norm_share, 'tp', axis=1, tiled=True)  84.5 us
    all_to_all x1, waiting for transfers between devices, body(): lax.all_to_all(returned_low, 'tok', split_axis=0, concat_axis=0, tiled=True)  66.1 us
    all_to_all x1, waiting for transfers between devices, body(): lax.all_to_all(feature_low, 'tok', split_axis=0, concat_axis=0, tiled=True)  64.3 us
    psum x1, waiting for transfers between devices, body(): lax.psum((d_qkv_weight, d_qv_bias, d_out_weight, d_out_bias, d_up_weight,...  63.2 us
  transfers between devices with their start and end apart: 10, of which 7 were waited for; matrix products, arithmetic and copies ran while one was open for 26% of the time, Pallas kernels for 0%

commit v1 on v0

v1 whole, which is shorter than its diff:
```python
import jax
import jax.numpy as jnp
from jax import lax
from jax.sharding import PartitionSpec as P

HD = 64
ROWS_DEV = 8
SLOTS = 289
EPSILON = 1e-06
MASKED_SCORE = -1000000000.0
BF = jnp.bfloat16
F32 = jnp.float32
EXACT = lax.Precision.HIGHEST


def ceil_to(value, step):
    return -(-value // step) * step


def normal_parts(values):
    row_mean = jnp.mean(values, axis=-1, keepdims=True)
    centered = values - row_mean
    inverse = lax.rsqrt(jnp.mean(centered * centered, axis=-1, keepdims=True) + EPSILON)
    return centered * inverse, inverse


def norm_back(grad_in, normal, inverse, gain_row):
    scaled = grad_in * gain_row
    return inverse * (
        scaled
        - jnp.mean(scaled, axis=-1, keepdims=True)
        - normal * jnp.mean(scaled * normal, axis=-1, keepdims=True)
    )


def mul(left, right):
    return lax.dot_general(left, right, (((1,), (0,)), ((), ())), preferred_element_type=F32)


def mul_t0(left, right):
    return lax.dot_general(left, right, (((0,), (0,)), ((), ())), preferred_element_type=F32)


def mul_t1(left, right):
    return lax.dot_general(left, right, (((1,), (1,)), ((), ())), preferred_element_type=F32)


def hot(rows, cols):
    return (rows[:, None] == cols[None, :]).astype(BF)


def columns_of(source, part, shares):
    width = source.shape[-1] // shares
    return lax.dynamic_slice_in_dim(source, part * width, width, source.ndim - 1)


def body(
    tokens,
    slot_index,
    segment,
    router,
    first_norm,
    qkv_weight,
    qv_bias,
    out_weight,
    out_bias,
    second_norm,
    up_weight,
    up_bias,
    down_weight,
    down_bias,
    cotangent,
):
    peers = lax.axis_size("tok")
    shares = lax.axis_size("tp")
    part = lax.axis_index("tp")
    half_bit = part % 2
    pair_bit = part // 2
    half_swap = [(i, i ^ 1) for i in range(shares)]
    pair_swap = [(i, i ^ 2) for i in range(shares)]
    count, width = tokens.shape
    inner = qkv_weight.shape[2]
    heads_local = inner // HD
    owned = ROWS_DEV * SLOTS
    live = owned - owned // 16
    capacity = -(-live // peers)
    quarter = -(-capacity // shares)
    block = ceil_to(quarter + 1, 8)
    picked = peers * block
    idle_share = -(-(count - live) // shares)
    idle = ceil_to(idle_share, 16)
    own = picked + idle

    chosen = slot_index >= 0
    owner = jnp.where(chosen, slot_index // owned, peers)
    lanes = jnp.arange(peers, dtype=jnp.int32)
    match = (owner[:, None] == lanes[None, :]).astype(jnp.int32)
    rank = jnp.sum(jnp.cumsum(match, axis=0) * match, axis=1) - 1
    idle_rank = jnp.cumsum(jnp.where(chosen, 0, 1)) - 1
    piece = rank // quarter
    offset = rank % quarter
    mine = chosen & (piece % 2 == half_bit)
    far = (piece // 2) ^ pair_bit
    send_row = jnp.where(mine, (owner * 2 + far) * block + offset, -1)
    picked_row = jnp.where(mine & (far == 0), owner * block + offset, -1)
    own_row = jnp.where(
        chosen,
        picked_row,
        jnp.where(idle_rank // idle_share == part, picked + idle_rank % idle_share, -1),
    )
    back_picked = jnp.where(chosen, piece * picked + owner * block + offset, -1)
    back_idle = jnp.where(chosen, -1, (idle_rank // idle_share) * idle + idle_rank % idle_share)

    up_all = lax.all_gather(up_weight, "tp")
    down_all = lax.all_gather(down_weight, "tp")

    send_hot = hot(jnp.arange(2 * picked, dtype=jnp.int32), send_row)
    own_hot = hot(jnp.arange(own, dtype=jnp.int32), own_row)
    send_in = mul(send_hot, tokens)
    send_hat, _ = normal_parts(send_in)
    send_rows = (send_hat * first_norm[0] + first_norm[1]).astype(BF)
    local_slot = jnp.where(chosen, slot_index % owned, 0)
    marks = jnp.stack([local_slot // 64 + 1, local_slot % 64, segment])
    block_of = jnp.where(mine, owner * 2 + far, -1)
    block_hot = (jnp.arange(2 * peers, dtype=jnp.int32)[:, None] == block_of[None, :])
    mark_left = jnp.where(block_hot[None], marks[:, None, :], 0).astype(BF)
    mark_right = hot(offset, jnp.arange(128, dtype=jnp.int32))
    mark_rows = mul(mark_left.reshape(6 * peers, count), mark_right).astype(BF)
    mark_rows = mark_rows.reshape(3, 2 * peers, 128).transpose(1, 0, 2).reshape(2 * peers, 1, 384)
    mark_rows = jnp.pad(mark_rows, ((0, 0), (0, 0), (0, width - 384)))
    row_kind = jnp.arange(block, dtype=jnp.int32)[None, :, None] == quarter
    send_rows = jnp.where(row_kind, mark_rows, send_rows.reshape(2 * peers, block, width))
    got_near = lax.all_to_all(
        send_rows.reshape(peers, 2, block, width), "tok", split_axis=0, concat_axis=0, tiled=True
    )
    got_far = lax.ppermute(got_near, "tp", half_swap)
    got = jnp.stack([got_near, got_far])
    mark = got[:, :, :, quarter, :].astype(jnp.int32)
    recv_slot = (mark[..., 0:block] - 1) * 64 + mark[..., 128 : 128 + block]
    recv_segment = mark[..., 256 : 256 + block]
    slot_rows = recv_slot.transpose(0, 2, 1, 3).reshape(4 * picked)
    segment_rows = recv_segment.transpose(0, 2, 1, 3).reshape(4 * picked)
    features = got.transpose(0, 2, 1, 3, 4).reshape(4 * picked, width)

    pad = 304
    ids = jnp.arange(ROWS_DEV * pad, dtype=jnp.int32)
    slot_ids = jnp.where(ids % pad < SLOTS, (ids // pad) * SLOTS + ids % pad, -1000)
    slot_hot = hot(slot_ids, slot_rows)
    slot_features = mul(slot_hot, features).astype(BF)
    flat_weight = qkv_weight.reshape(width, 3 * inner)
    bias_row = jnp.concatenate([qv_bias[0], jnp.zeros_like(qv_bias[0]), qv_bias[1]])
    slot_qkv = (mul(slot_features, flat_weight) + bias_row).astype(BF)
    slot_segment = (
        jnp.sum(jnp.where(slot_hot > 0, segment_rows[None, :] + 1, 0), axis=1) - 1
    ).reshape(ROWS_DEV, pad)
    allowed = (slot_segment[:, :, None] == slot_segment[:, None, :]) & (
        slot_segment[:, None, :] >= 0
    )
    grouped = slot_qkv.reshape(ROWS_DEV, pad, 3, heads_local, HD)
    query, key, value = grouped[:, :, 0], grouped[:, :, 1], grouped[:, :, 2]
    score_scale = HD ** (-0.5)
    scores = (
        jnp.einsum("rqhe,rkhe->rhqk", query, key, preferred_element_type=F32) * score_scale
    )
    scores = jnp.where(allowed[:, None], scores, MASKED_SCORE)
    top = jnp.max(scores, axis=-1, keepdims=True)
    raised = jnp.exp(scores - top)
    weights = raised / jnp.sum(raised, axis=-1, keepdims=True)
    weights_low = weights.astype(BF)
    attended = jnp.einsum("rhqk,rkhe->rqhe", weights_low, value, preferred_element_type=F32)
    heads = attended.reshape(ROWS_DEV * pad, inner).astype(BF)
    heads_rows = mul_t0(slot_hot, heads).astype(BF)
    bias_full = lax.dynamic_update_slice(
        jnp.zeros((width,), F32), out_bias, (part * (width // shares),)
    )

    def share_sum(partial):
        near, far_half = partial[: 2 * picked], partial[2 * picked :]
        got_half = lax.ppermute(far_half.astype(BF), "tp", half_swap)
        joined = near + got_half.astype(F32)
        got_pair = lax.ppermute(joined[picked:].astype(BF), "tp", pair_swap)
        return (joined[:picked] + got_pair.astype(F32)).astype(BF)

    def across(rows):
        return lax.all_to_all(
            rows.reshape(peers, block, width), "tok", split_axis=0, concat_axis=0, tiled=True
        ).reshape(picked, width)

    returned = across(share_sum(mul(heads_rows, out_weight) + bias_full))

    own_in = mul(own_hot, tokens)
    own_cot_low = mul(own_hot, cotangent).astype(BF)
    own_cot = own_cot_low.astype(F32)
    gate = jax.nn.sigmoid(jnp.dot(own_in, router, precision=EXACT))
    branch = jnp.pad(returned.astype(F32), ((0, idle), (0, 0)))
    scale = jnp.where(jnp.arange(own) < picked, gate, 0.0)
    residual = own_in + scale[:, None] * branch
    second_hat, second_inv = normal_parts(residual)
    second = (second_hat * second_norm[0] + second_norm[1]).astype(BF)
    up_cols = up_all.transpose(1, 0, 2).reshape(width, -1)
    down_rows = down_all.reshape(-1, width)
    up_bias_all = lax.all_gather(up_bias, "tp", tiled=True)
    down_bias_all = lax.all_gather(down_bias, "tp", tiled=True)
    pre = mul(second, up_cols) + up_bias_all
    below = 0.5 * (1.0 + lax.erf(pre * (2.0**-0.5)))
    bell = jnp.exp(-0.5 * pre * pre) * (2.0 * jnp.pi) ** -0.5
    hidden = (pre * below).astype(BF)
    layer_rows = (residual + mul(hidden, down_rows) + down_bias_all).astype(BF)
    d_hidden = mul_t1(own_cot_low, down_rows)
    d_pre = (d_hidden * (below + pre * bell)).astype(BF)
    d_down = mul_t0(hidden, own_cot_low).astype(BF).reshape(shares, -1, width)
    d_up = mul_t0(second, d_pre).astype(BF)
    d_up = d_up.reshape(width, shares, -1).transpose(1, 0, 2)
    d_second = mul_t1(d_pre, up_cols)
    d_residual = own_cot + norm_back(d_second, second_hat, second_inv, second_norm[0])
    d_branch = (d_residual[:picked] * scale[:picked, None]).astype(BF)
    d_logit = jnp.sum(d_residual * branch, axis=1) * scale * (1.0 - gate)
    small = jnp.concatenate(
        [
            jnp.sum(d_pre.astype(F32), axis=0).reshape(shares, width),
            jnp.stack(
                [
                    jnp.sum(d_second * second_hat, axis=0),
                    jnp.sum(d_second, axis=0),
                    jnp.sum(own_cot, axis=0),
                    jnp.sum(d_branch.astype(F32), axis=0),
                    jnp.sum(d_logit[:, None] * own_in, axis=0),
                ]
            ),
        ]
    )
    d_up_share = lax.psum_scatter(d_up, "tp", scatter_dimension=0)
    d_down_share = lax.psum_scatter(d_down, "tp", scatter_dimension=0)
    d_up_total = lax.psum(d_up_share, "tok").astype(F32)
    d_down_total = lax.psum(d_down_share, "tok").astype(F32)

    grad_own = across(d_branch)
    grad_near = jnp.concatenate([grad_own, lax.ppermute(grad_own, "tp", pair_swap)])
    grad_rows = jnp.concatenate([grad_near, lax.ppermute(grad_near, "tp", half_swap)])
    d_out_weight = mul_t0(heads_rows, grad_rows)
    d_heads_rows = mul_t1(grad_rows, out_weight).astype(BF)
    d_heads = mul(slot_hot, d_heads_rows).astype(BF).reshape(ROWS_DEV, pad, heads_local, HD)
    d_weights = jnp.einsum("rqhe,rkhe->rhqk", d_heads, value, preferred_element_type=F32)
    d_value = jnp.einsum("rhqk,rqhe->rkhe", weights_low, d_heads, preferred_element_type=F32)
    d_scores = (
        weights * (d_weights - jnp.sum(weights * d_weights, axis=-1, keepdims=True))
    ).astype(BF)
    d_query = (
        jnp.einsum("rhqk,rkhe->rqhe", d_scores, key, preferred_element_type=F32) * score_scale
    )
    d_key = (
        jnp.einsum("rhqk,rqhe->rkhe", d_scores, query, preferred_element_type=F32) * score_scale
    )
    d_qkv = (
        jnp.stack([d_query, d_key, d_value], axis=2).astype(BF).reshape(ROWS_DEV * pad, 3 * inner)
    )
    d_qkv_weight = mul_t0(slot_features, d_qkv)
    d_qkv_bias = jnp.sum(d_qkv.astype(F32), axis=0).reshape(3, inner)
    d_qv_bias = jnp.stack([d_qkv_bias[0], d_qkv_bias[2]])
    d_qkv_rows = mul_t0(slot_hot, d_qkv).astype(BF)
    d_normed = across(share_sum(mul_t1(d_qkv_rows, flat_weight))).astype(F32)
    d_qkv_total = lax.psum(d_qkv_weight.astype(BF), "tok").astype(F32)
    d_out_total = lax.psum(d_out_weight.astype(BF), "tok").astype(F32)

    first_hat, first_inv = normal_parts(own_in[:picked])
    d_picked = (
        d_residual[:picked]
        + norm_back(d_normed, first_hat, first_inv, first_norm[0])
        + d_logit[:picked, None] * router[None, :]
    ).astype(BF)
    d_idle = d_residual[picked:].astype(BF)

    def to_columns(rows):
        pieces = rows.reshape(rows.shape[0], shares, width // shares).transpose(1, 0, 2)
        return lax.all_to_all(pieces, "tp", split_axis=0, concat_axis=0, tiled=True).reshape(
            shares * rows.shape[0], width // shares
        )

    picked_hot = hot(back_picked, jnp.arange(shares * picked, dtype=jnp.int32))
    idle_hot = hot(back_idle, jnp.arange(shares * idle, dtype=jnp.int32))
    layer_out = (
        mul(picked_hot, to_columns(layer_rows[:picked]))
        + mul(idle_hot, to_columns(layer_rows[picked:]))
    ).astype(BF)
    d_tokens = mul(picked_hot, to_columns(d_picked)) + mul(idle_hot, to_columns(d_idle))
    first_pair = jnp.stack([jnp.sum(d_normed * first_hat, axis=0), jnp.sum(d_normed, axis=0)])
    small = lax.psum(jnp.concatenate([small, first_pair]), ("tok", "tp"))
    small_cols = columns_of(small[shares:], part, shares)
    d_up_bias = lax.dynamic_slice_in_dim(small, part, 1, 0).reshape(width)
    d_qv_bias = lax.psum(d_qv_bias, "tok")
    return (
        layer_out,
        d_tokens,
        d_qkv_total.reshape(width, 3, inner),
        d_qv_bias,
        d_out_total,
        small_cols[3],
        d_up_total,
        d_up_bias,
        d_down_total,
        small_cols[2],
        small_cols[5:7],
        small_cols[0:2],
        small_cols[4],
    )


def solution(mesh):
    return jax.shard_map(
        body,
        mesh=mesh,
        in_specs=(
            P("tok", None),
            P("tok"),
            P("tok"),
            P(),
            P(),
            P(None, None, "tp"),
            P(None, "tp"),
            P("tp", None),
            P("tp"),
            P(),
            P(None, "tp"),
            P("tp"),
            P("tp", None),
            P("tp"),
            P("tok", None),
        ),
        out_specs=(
            P("tok", "tp"),
            P("tok", "tp"),
            P(None, None, "tp"),
            P(None, "tp"),
            P("tp", None),
            P("tp"),
            P(None, "tp"),
            P("tp"),
            P("tp", None),
            P("tp"),
            P(None, "tp"),
            P(None, "tp"),
            P("tp"),
        ),
        check_vma=False,
    )
```

time: 1570 us -> 705 us (0.45)
  waiting for transfers between devices: 480 us -> 72.8 us
  local copies, waits for them, and re-layouts: 390 us -> 80.1 us
  other arithmetic: 197 us -> 63.7 us
  blocking collectives: 281 us -> 175 us
  matrix products: 164 us -> 260 us
  starting transfers between devices: 45.6 us -> 29.2 us
    psum x3 -> x2, blocking collectives: 281 us -> 61.9 us  [the longest x1 38.3 us: body(): small = lax.psum(jnp.concatenate([small, first_pair]), ('tok', 'tp'))]
    all_to_all x6, waiting for transfers between devices: 221 us -> 16.4 us  [the longest x4 14.8 us: to_columns(): lax.all_to_all(pieces, 'tp', split_axis=0, concat_axis=0, tiled=True)]
    gather x19 -> x0, local copies, waits for them, and re-layouts: 199 us -> none  [the longest x15 137 us: pick_rows(): return jnp.take(source, index_rows, axis=0, mode='fill', fill_value=filler)]
    reduce_scatter x2, waiting for transfers between devices: 111 us -> 0.03 us  [the longest x1 0.02 us: body(): d_up_share = lax.psum_scatter(d_up, 'tp', scatter_dimension=0)]
    dot_general x20 -> x28, matrix products: 164 us -> 251 us  [the longest x14 149 us: mul(): lax.dot_general(left, right, (((1,), (0,)), ((), ())), preferred_element_...]
    all_gather x1 -> x2, waiting for transfers between devices: 84.5 us -> 0.02 us  [the longest x1 0.02 us: body(): down_all = lax.all_gather(down_weight, 'tp')]
    all_to_all x0 -> x2, blocking collectives: none -> 75.3 us  [the longest x1 48.4 us: body(): lax.all_to_all(send_rows.reshape(peers, 2, block, width), 'tok', split_ax...]
    reduce_sum x13, other arithmetic: 88.7 us -> 22.5 us  [the longest x2 4.45 us: normal_parts(): row_mean = jnp.mean(values, axis=-1, keepdims=True)]
  transfers between devices with their start and end apart: 10 -> 18, of which waited for: 7 -> 7; matrix products, arithmetic and copies ran while one was open for 26% -> 52% of each run, Pallas kernels for 0% -> 0%
where the time goes in v1:
time: 705 us; the launch traced here: 696 us
  matrix products  260 us (37%)
  blocking collectives  175 us (25%)
  local copies, waits for them, and re-layouts  80.1 us (11%)
  waiting for transfers between devices  72.8 us (10%)
  other arithmetic  63.7 us (9%)
  starting transfers between devices  29.2 us (4%)
  between operations  16 us (2%)
    dot_general x14, matrix products, mul(): lax.dot_general(left, right, (((1,), (0,)), ((), ())), preferred_element_...  149 us
    all_to_all x1, blocking collectives, body(): lax.all_to_all(send_rows.reshape(peers, 2, block, width), 'tok', split_ax...  48.4 us
    dot_general x3, matrix products, mul_t1(): lax.dot_general(left, right, (((1,), (1,)), ((), ())), preferred_element_...  44.5 us
    psum x1, waiting for transfers between devices, body(): d_qkv_total = lax.psum(d_qkv_weight.astype(BF), 'tok').astype(F32)  42.6 us
    psum x1, blocking collectives, body(): small = lax.psum(jnp.concatenate([small, first_pair]), ('tok', 'tp'))  38.3 us
    dot_general x5, matrix products, mul_t0(): lax.dot_general(left, right, (((0,), (0,)), ((), ())), preferred_element_...  30.6 us
    all_to_all x1, blocking collectives, across(): lax.all_to_all(rows.reshape(peers, block, width), 'tok', split_axis=0, co...  26.9 us
    psum x1, blocking collectives, body(): d_qv_bias = lax.psum(d_qv_bias, 'tok')  23.6 us
  transfers between devices with their start and end apart: 18, of which 7 were waited for; matrix products, arithmetic and copies ran while one was open for 52% of the time, Pallas kernels for 0%

profile of v1, /device:TPU:0, one launch (start us, length us, event | category | flops | bytes accessed | tf_op | source)
XLA Modules:
  0.0 696.4 jit_solution(4545855774942127467)
XLA Ops:
  16.0 14.7 %fusion.135 = (f32[1152]{0:T(1024)S(1)}, f32[1152,768]{1,0:T(8,128)S(1)}) fusion(bf16[4616,768]{1,0:T(8,128)(2,1)} %param.15, s32[4616]{0:T(1024)S(1)} %get-tuple-element.46), kind=kOutput, calls=%fused_computation.269 | convolution fusion | flops 8174084096 | bytes 10652192 | tf_op jit(solution)/shard_map/dot_general | solution.py:37
  32.1 48.4 %all_to_all.40 = bf16[8,2,72,768]{3,2,1,0:T(8,128)(2,1)S(1)} all-to-all(bf16[8,2,72,768]{3,2,1,0:T(8,128)(2,1)S(1)} %broadcast_select_fusion), channel_id=1, replica_groups=mesh['tok'=8,'tp'=4] {'tok'}, dimensions={0} | all-to-all | bytes 3538944 | tf_op jit(solution)/shard_map/all_to_all | solution.py:133
  89.7 12.9 %fusion.44 = bf16[2432,768]{1,0:T(8,128)(2,1)} fusion(bf16[2304,768]{1,0:T(8,128)(2,1)} %bitcast.217, s32[2304]{0:T(1024)S(1)} %eq.201, s32[2432]{0:T(1024)S(1)} %fusion.120), kind=kOutput, calls=%fused_computation.64 | convolution fusion | flops 8614182912 | bytes 7293440 | tf_op jit(solution)/shard_map/dot_general | solution.py:37
  158.5 15.3 %fusion.16 = f32[1200,768]{1,0:T(8,128)S(1)} fusion(bf16[4616,768]{1,0:T(8,128)(2,1)} %param.15, s32[4616]{0:T(1024)S(1)} %get-tuple-element.47), kind=kOutput, calls=%fused_computation.20 | convolution fusion | flops 8513750528 | bytes 10795040 | tf_op jit(solution)/shard_map/dot_general | solution.py:37
  179.0 20.1 %all-gather.2 = f32[4,1,768]{2,1,0:T(1,128)S(1)} all-gather(f32[1,1,768]{2,1,0:T(1,128)S(1)} %reshape.375), channel_id=1, replica_groups=mesh['tok'=8,'tp'=4] {'tp'}, dimensions={0}, use_global_device_ids=true | all-gather | bytes 15360 | tf_op jit(solution)/shard_map/all_gather | solution.py:202
  203.8 14.6 %fusion.65 = bf16[1200,768]{1,0:T(8,128)(2,1)} fusion(bf16[4616,768]{1,0:T(8,128)(2,1)} %param.29, s32[4616]{0:T(1024)S(1)} %get-tuple-element.47), kind=kOutput, calls=%fused_computation.100 | convolution fusion | flops 8514672128 | bytes 8951840 | tf_op jit(solution)/shard_map/dot_general | solution.py:37
  231.3 10.5 %multiply_convert_fusion = (bf16[1200,3072]{1,0:T(8,128)(2,1)S(1)}, f32[1200,3072]{1,0:T(8,128)}) fusion(f32[3072]{0:T(1024)S(1)} %bitcast.228, bf16[768,3072]{0,1:T(8,128)(2,1)S(1)} %bitcast.209, f32[768]{0:T(1024)S(1)} %get-tuple-element.24, f32[768]{0:T(1024)S(1)} %get-tuple-element.23, f32[1200]{0:T(1024)S(1)} %add_rsqrt_fusion, ...), kind=kOutput, calls=%fused_computation.34 | convolution fusion | flops 5691801600 | bytes 31440960 | tf_op jit(solution)/shard_map/dot_general | solution.py:37
  241.8 8.3 %convolution_convert_fusion = bf16[3072,768]{1,0:T(8,128)(2,1)} fusion(bf16[1200,3072]{1,0:T(8,128)(2,1)S(1)} %get-tuple-element.67, bf16[1200,768]{1,0:T(8,128)(2,1)S(1)} %copy-done.16), kind=kOutput, calls=%fused_computation.65 | convolution fusion | flops 5664669696 | bytes 13934592 | tf_op jit(solution)/shard_map/dot_general | solution.py:41
  250.2 14.4 %convert_reduce_fusion = (f32[3072]{0:T(1024)}, bf16[1200,3072]{1,0:T(8,128)(2,1)S(1)}) fusion(f32[1200,3072]{1,0:T(8,128)} %get-tuple-element.68, bf16[1200,768]{1,0:T(8,128)(2,1)} %fusion.65, bf16[3072,768]{1,0:T(8,128)(2,1)} %all-gather.8.cloned.1.call-done), kind=kOutput, calls=%fused_computation.33 | convolution fusion | flops 5706544128 | bytes 28692480 | tf_op jit(solution)/shard_map/dot_general | solution.py:45
  264.6 13.5 %multiply_reduce_fusion.2 = (f32[768]{0:T(1024)}, f32[1200]{0:T(1024)S(1)}, f32[1200]{0:T(1024)S(1)}, f32[768]{0:T(1024)}, f32[1200,768]{1,0:T(8,128)S(1)}) fusion(f32[1200]{0:T(1024)S(1)} %add_rsqrt_fusion, f32[1200]{0:T(1024)S(1)} %broadcast_multiply_fusion.2, f32[1200,768]{1,0:T(8,128)S(1)} %copy-done.3, bf16[576,768]{1,0:T(8,128)(2,1)S(1)} %bitcast.199, ...), kind=kOutput, calls=%fused_computation.86 | convolution fusion | flops 5673365504 | bytes 20382144 | tf_op jit(solution)/shard_map/dot_general | solution.py:45
  284.9 26.9 %all_to_all.41 = bf16[8,72,768]{2,1,0:T(8,128)(2,1)S(1)} all-to-all(bf16[8,72,768]{2,1,0:T(8,128)(2,1)S(1)} %bitcast.218), channel_id=1, replica_groups=mesh['tok'=8,'tp'=4] {'tok'}, dimensions={0} | all-to-all | bytes 1769472 | tf_op jit(solution)/shard_map/all_to_all | solution.py:185
  317.3 17.7 %all-reduce.4 = f32[768]{0:T(1024)} all-reduce(f32[768]{0:T(1024)} %dynamic-update-slice), channel_id=1, replica_groups=mesh['tok'=8,'tp'=4] {'tp'}, use_global_device_ids=true, to_apply=%add.4 | all-reduce | flops 768 | bytes 6144
  336.4 10.9 %convolution_convert_fusion.1 = bf16[768,3072]{1,0:T(8,128)(2,1)S(1)} fusion(bf16[1200,3072]{1,0:T(8,128)(2,1)} %copy-done.52, f32[768]{0:T(1024)} %copy-done.45, f32[768]{0:T(1024)} %copy-done.34, f32[1200]{0:T(1024)} %copy-done.31, f32[1200]{0:T(1024)S(1)} %broadcast_multiply_fusion.2, f32[1200,768]{1,0:T(8,128)} %copy-done.1, ...), kind=kOutput, calls=%fused_computation.66 | convolution fusion | flops 5672042496 | bytes 16683072 | tf_op jit(solution)/shard_map/dot_general | solution.py:41
  366.7 8.9 %multiply_reduce_fusion = (f32[8,3,304]{2,1,0:T(4,128)S(1)}, f32[8,3,304,304]{2,3,1,0:T(8,128)}) fusion(f32[8,3,304,304]{2,3,1,0:T(8,128)} %get-tuple-element.66, f32[8,3,304]{2,1,0:T(4,128)S(1)} %copy-done.29, bf16[8,304,1,3,64]{1,0,4,3,2:T(8,128)(2,1)S(1)} %copy-done.18, bf16[8,304,3,64]{1,0,3,2:T(8,128)(2,1)S(1)} %reshape.354), kind=kOutput, calls=%fused_computation.40 | convolution fusion | flops 290548608 | bytes 19670016 | tf_op jit(solution)/shard_map/rqhe,rkhe->rhqk/dot_general | solution.py:243
  396.8 16.6 %fusion.62 = f32[2304,768]{1,0:T(8,128)} fusion(bf16[768,576]{0,1:T(8,128)(2,1)S(1)} %bitcast.192, bf16[2432,576]{0,1:T(8,128)(2,1)} %convert_element_type.200, s32[2304]{0:T(1024)S(1)} %copy-done.40, s32[2432]{0:T(1024)S(1)} %copy-done.42), kind=kOutput, calls=%fused_computation.98 | convolution fusion | flops 8500396032 | bytes 10783232 | tf_op jit(solution)/shard_map/dot_general | solution.py:45
  417.5 10.6 %fusion.64 = bf16[1200,768]{1,0:T(8,128)(2,1)S(1)} fusion(bf16[1200,3072]{1,0:T(8,128)(2,1)} %copy-done.54, bf16[3072,768]{1,0:T(8,128)(2,1)} %all-gather.8.cloned.1.call-done, f32[768]{0:T(1024)S(1)} %copy-done.49, f32[1200,768]{1,0:T(8,128)} %copy-done.1, bf16[576,768]{1,0:T(8,128)(2,1)S(1)} %bitcast.202, f32[1200]{0:T(1024)S(1)} %fusion.123), kind=kOutput, calls=%fused_computation.99 | convolution fusion | flops 5667840000 | bytes 18513600 | tf_op jit(solution)/shard_map/dot_general | solution.py:37
  437.3 10.7 %all-to-all-done.2 = bf16[4,576,192]{1,2,0:T(8,128)(2,1)S(1)} async-done(((bf16[4,576,192]{1,2,0:T(8,128)(2,1)}), bf16[4,576,192]{1,2,0:T(8,128)(2,1)S(1)}, u32[]{:S(2)}, u32[]{:S(2)}) %all-to-all-start.2) | async-done | bytes 884768 | tf_op jit(solution)/shard_map/all_to_all | solution.py:275
  482.7 13.4 %fusion.2 = f32[4616,192]{0,1:T(8,128)} fusion(bf16[2496,192]{0,1:T(8,128)(2,1)} %reshape.351, s32[4616]{0:T(1024)S(1)} %copy-done.33), kind=kOutput, calls=%fused_computation.3 | convolution fusion | flops 4435791360 | bytes 4522016 | tf_op jit(solution)/shard_map/dot_general | solution.py:37
  510.3 13.9 %fusion.40 = bf16[4616,192]{0,1:T(8,128)(2,1)} fusion(f32[4616,192]{0,1:T(8,128)} %fusion.2, bf16[2304,192]{0,1:T(8,128)(2,1)} %reshape.349, s32[4616]{0:T(1024)S(1)} %copy-done.32), kind=kOutput, calls=%fused_computation.57 | convolution fusion | flops 4096349184 | bytes 6220832 | tf_op jit(solution)/shard_map/dot_general | solution.py:37
  546.9 13.5 %fusion.1 = f32[4616,192]{0,1:T(8,128)} fusion(bf16[2496,192]{0,1:T(8,128)(2,1)} %reshape.359, s32[4616]{0:T(1024)S(1)} %copy-done.33), kind=kOutput, calls=%fused_computation.2 | convolution fusion | flops 4435791360 | bytes 4522016 | tf_op jit(solution)/shard_map/dot_general | solution.py:37
  560.6 23.6 %psum.43 = f32[2,192]{1,0:T(2,128)} all-reduce(f32[2,192]{1,0:T(2,128)S(1)} %pad_maximum_fusion.8), channel_id=1, replica_groups=mesh['tok'=8,'tp'=4] {'tok'}, use_global_device_ids=true, to_apply=%region_22.23 | all-reduce | flops 384 | bytes 3072 | tf_op jit(solution)/shard_map/psum | solution.py:290
  584.3 38.3 %psum.45 = f32[11,768]{1,0:T(8,128)S(1)} all-reduce(f32[11,768]{1,0:T(8,128)S(1)} %concatenate.16), channel_id=1, replica_groups=mesh['tok'=8,'tp'=4] {'tok','tp'}, use_global_device_ids=true, to_apply=%region_32.33 | all-reduce | flops 8448 | bytes 67584 | tf_op jit(solution)/shard_map/psum | solution.py:287
  625.9 13.6 %fusion.39 = f32[4616,192]{0,1:T(8,128)} fusion(f32[4616,192]{0,1:T(8,128)} %fusion.1, bf16[2304,192]{0,1:T(8,128)(2,1)S(1)} %reshape.357, s32[4616]{0:T(1024)S(1)} %copy-done.32), kind=kOutput, calls=%fused_computation.56 | convolution fusion | flops 4095462912 | bytes 7993376 | tf_op jit(solution)/shard_map/dot_general | solution.py:37
  639.5 42.6 %all-reduce.8.cloned.1.call-done = (bf16[768,3,192]{0,2,1:T(8,128)(2,1)}, bf16[192,768]{1,0:T(8,128)(2,1)}, bf16[768,768]{1,0:T(8,128)(2,1)}, bf16[768,768]{1,0:T(8,128)(2,1)}) async-done(((bf16[768,3,192]{0,2,1:T(8,128)(2,1)}, bf16[192,768]{1,0:T(8,128)(2,1)}, bf16[768,768]{1,0:T(8,128)(2,1)}, bf16[768,768]{1,0:T(8,128)(2,1)}), (bf16[768,3,192]{0,2,1:T(8,128)(2,1)}, bf16[192,768]{1,0:T(8,128)(2,1)}, ...) | async-done | bytes 3538960 | tf_op jit(solution)/shard_map/psum | solution.py:262
  (309 shorter events, 246.6 us)
Async XLA Ops:
  7.2 99.4 %copy-start = (bf16[768,3,192]{0,2,1:T(8,128)(2,1)S(1)}, bf16[768,3,192]{0,2,1:T(8,128)(2,1)}, u32[]{:S(2)}) copy-start(bf16[768,3,192]{0,2,1:T(8,128)(2,1)} %param.20) | copy-start | bytes 2654212
  7.2 211.3 %all-gather.6.cloned.1.call-start = ((), (), s32[]{:S(2)}) async-start(), calls=%async_computation.12 | async-start | bytes 5898240 | tf_op jit(solution)/shard_map/all_gather | solution.py:114
  32.1 48.9 %copy-start.51 = (f32[192]{0:T(256)S(1)}, f32[192]{0:T(256)}, u32[]{:S(2)}) copy-start(f32[192]{0:T(256)} %param.23) | copy-start | bytes 2308
  32.1 49.1 %copy-start.50 = (f32[2,192]{1,0:T(2,128)S(1)}, f32[2,192]{1,0:T(2,128)}, u32[]{:S(2)}) copy-start(f32[2,192]{1,0:T(2,128)} %param.21) | copy-start | bytes 4612
  80.6 3.9 collective-permute-start
  80.7 169.5 %all-gather.8.cloned.1.call-start = ((), (), s32[]{:S(2)}) async-start(), calls=%async_computation.13 | async-start | bytes 5898240 | tf_op jit(solution)/shard_map/all_gather | solution.py:115
  81.3 60.2 %copy-start.41 = (s32[2432]{0:T(1024)}, s32[2432]{0:T(1024)S(1)}, u32[]{:S(2)}) copy-start(s32[2432]{0:T(1024)S(1)} %fusion.120) | copy-start | bytes 29188
  89.7 51.8 %copy-start.39 = (s32[2304]{0:T(1024)}, s32[2304]{0:T(1024)S(1)}, u32[]{:S(2)}) copy-start(s32[2304]{0:T(1024)S(1)} %eq.201) | copy-start | bytes 27652
  149.9 3.9 collective-permute-start.1
  157.2 42.0 %collective-permute-start.2 = (bf16[576,768]{1,0:T(8,128)(2,1)S(1)}, bf16[576,768]{1,0:T(8,128)(2,1)S(1)}, u32[]{:S(2)}, u32[]{:S(2)}) collective-permute-start(bf16[576,768]{1,0:T(8,128)(2,1)S(1)} %slice.292), channel_id=1, source_target_pairs={{0,2},{1,3},{2,0},{3,1},{4,6},{5,7},{6,4},{7,5},{8,10},{9,11},{10,... | collective-permute-start | bytes 2654216 | tf_op jit(solution)/shard_map/ppermute | solution.py:181
  199.1 79.0 %copy-start.34 = (f32[768]{0:T(1024)}, f32[768]{0:T(1024)S(1)}, u32[]{:S(2)}) copy-start(f32[768]{0:T(1024)S(1)} %get-tuple-element.23) | copy-start | bytes 9220
  200.2 26.5 %all-to-all-start.1 = ((bf16[8,72,768]{2,1,0:T(8,128)(2,1)}), bf16[8,72,768]{2,1,0:T(8,128)(2,1)S(1)}, u32[]{:S(2)}, u32[]{:S(2)}) async-start(bf16[8,72,768]{2,1,0:T(8,128)(2,1)} %bitcast.21), calls=%async_computation.1 | async-start | bytes 1769472 | tf_op jit(solution)/shard_map/all_to_all | solution.py:185
  203.8 335.3 %reduce-scatter.5.cloned.1.call-start = ((), (), s32[]{:S(2)}) async-start(), calls=%async_computation.11 | async-start | bytes 5898240 | tf_op jit(solution)/shard_map/reduce_scatter | solution.py:233
  250.2 288.9 %reduce-scatter.3.cloned.1.call-start = ((), (), s32[]{:S(2)}) async-start(), calls=%async_computation.10 | async-start | bytes 5898240 | tf_op jit(solution)/shard_map/reduce_scatter | solution.py:232
  311.8 23.2 %collective-permute-start.3 = (bf16[576,768]{1,0:T(8,128)(2,1)S(1)}, bf16[576,768]{1,0:T(8,128)(2,1)S(1)}, u32[]{:S(2)}, u32[]{:S(2)}) collective-permute-start(bf16[576,768]{1,0:T(8,128)(2,1)S(1)} %bitcast.212), channel_id=1, source_target_pairs={{0,2},{1,3},{2,0},{3,1},{4,6},{5,7},{6,4},{7,5},{8,10},{9,11},{10,... | collective-permute-start | bytes 2654216 | tf_op jit(solution)/shard_map/ppermute | solution.py:238
  336.4 13.4 %collective-permute-start.4 = (bf16[1152,768]{1,0:T(8,128)(2,1)}, bf16[1152,768]{1,0:T(8,128)(2,1)}, u32[]{:S(2)}, u32[]{:S(2)}) collective-permute-start(bf16[1152,768]{1,0:T(8,128)(2,1)} %pad_maximum_fusion.2), channel_id=1, source_target_pairs={{0,1},{1,0},{2,3},{3,2},{4,5},{5,4},{6,7},{7,6},{8,9},{9,8},{10,11... | collective-permute-start | bytes 5308424 | tf_op jit(solution)/shard_map/ppermute | solution.py:239
  417.0 58.1 %collective-permute-start.5 = (bf16[1152,768]{1,0:T(8,128)(2,1)}, bf16[1152,768]{1,0:T(8,128)(2,1)}, u32[]{:S(2)}, u32[]{:S(2)}) collective-permute-start(bf16[1152,768]{1,0:T(8,128)(2,1)} %slice.288), channel_id=1, source_target_pairs={{0,1},{1,0},{2,3},{3,2},{4,5},{5,4},{6,7},{7,6},{8,9},{9,8},{10,11... | collective-permute-start | bytes 5308424 | tf_op jit(solution)/shard_map/ppermute | solution.py:179
  430.7 17.2 %all-to-all-start.2 = ((bf16[4,576,192]{1,2,0:T(8,128)(2,1)}), bf16[4,576,192]{1,2,0:T(8,128)(2,1)S(1)}, u32[]{:S(2)}, u32[]{:S(2)}) async-start(bf16[4,576,192]{1,2,0:T(8,128)(2,1)} %bitcast.29), calls=%async_computation.2 | async-start | bytes 1966080 | tf_op jit(solution)/shard_map/all_to_all | solution.py:275
  447.9 18.1 %all-to-all-start.3 = ((bf16[4,624,192]{1,2,0:T(8,128)(2,1)}), bf16[4,624,192]{1,2,0:T(8,128)(2,1)}, u32[]{:S(2)}, u32[]{:S(2)}) async-start(bf16[4,624,192]{1,2,0:T(8,128)(2,1)} %bitcast.31), calls=%async_computation.3 | async-start | bytes 1966080 | tf_op jit(solution)/shard_map/all_to_all | solution.py:275
  466.0 39.6 %all-to-all-start.7 = ((bf16[4,624,192]{1,2,0:T(8,128)(2,1)}), bf16[4,624,192]{1,2,0:T(8,128)(2,1)S(1)}, u32[]{:S(2)}, u32[]{:S(2)}) async-start(bf16[4,624,192]{1,2,0:T(8,128)(2,1)} %bitcast.211), calls=%async_computation.7 | async-start | bytes 1966080 | tf_op jit(solution)/shard_map/all_to_all | solution.py:275
  480.8 22.2 %collective-permute-start.6 = (bf16[576,768]{1,0:T(8,128)(2,1)}, bf16[576,768]{1,0:T(8,128)(2,1)S(1)}, u32[]{:S(2)}, u32[]{:S(2)}) collective-permute-start(bf16[576,768]{1,0:T(8,128)(2,1)} %slice.291), channel_id=1, source_target_pairs={{0,2},{1,3},{2,0},{3,1},{4,6},{5,7},{6,4},{7,5},{8,10},{9,11},{10,... | collective-permute-start | bytes 2654216 | tf_op jit(solution)/shard_map/ppermute | solution.py:181
  505.6 30.7 %all-to-all-start.5 = ((bf16[8,72,768]{2,1,0:T(8,128)(2,1)}), bf16[8,72,768]{2,1,0:T(8,128)(2,1)S(1)}, u32[]{:S(2)}, u32[]{:S(2)}) async-start(bf16[8,72,768]{2,1,0:T(8,128)(2,1)} %bitcast.216), calls=%async_computation.5 | async-start | bytes 1769472 | tf_op jit(solution)/shard_map/all_to_all | solution.py:185
  510.3 171.8 %all-reduce.8.cloned.1.call-start = ((), (), s32[]{:S(2)}) async-start(), calls=%async_computation.14 | async-start | bytes 7077888 | tf_op jit(solution)/shard_map/psum | solution.py:262
  543.0 81.5 %all-to-all-start.6 = ((bf16[4,576,192]{1,2,0:T(8,128)(2,1)}), bf16[4,576,192]{1,2,0:T(8,128)(2,1)S(1)}, u32[]{:S(2)}, u32[]{:S(2)}) async-start(bf16[4,576,192]{1,2,0:T(8,128)(2,1)} %bitcast.43), calls=%async_computation.6 | async-start | bytes 1966080 | tf_op jit(solution)/shard_map/all_to_all | solution.py:275
  (54 other events, 616.6 us)
Sparse Core Ops, SparseCore 0:
  80.8 36.5 all-gather.5
  150.1 55.5 all-gather.7
  250.3 47.4 reduce-scatter.4
  350.0 46.9 reduce-scatter.2
  539.3 142.7 all-reduce.7
